TPU v7x, 32 devices: a whole 2x2x4 slice. The times are simulated.
32 devices in a mesh: ctx: 8 (over z, y), fsdp: 4 (over x, core).
Axes of the slice: x: 2, y: 2, z: 4, core: 2. Of those that a mesh axis runs over, the one named last changes fastest.
Arguments:
- queries: bfloat16 [4, 3072, 1024], P('fsdp', 'ctx'), may hold values from -27 to 27
- keys: bfloat16 [4, 3072, 1024], P('fsdp', 'ctx'), may hold values from -27 to 27
- values: bfloat16 [4, 3072, 1024], P('fsdp', 'ctx'), may hold values from -6 to 6
- upstream: bfloat16 [4, 3072, 2048], P('fsdp', 'ctx'), may hold values from -6 to 6
- out_weight: bfloat16 [1024, 2048], P('fsdp'), may hold values from -0.1875 to 0.1875
- slopes: float32 [8], replicated, may hold values from 0.002 to 0.05
- patch_index: int32 [4, 3072], P('fsdp'), may hold values from 0 to 9213, as said below
- pair_lists: int32 [4, 2, 360], P('fsdp', None, 'ctx'), may hold values from 0 to 14, as said below
- pair_counts: int32 [4, 8], P('fsdp', 'ctx'), may hold values from 3 to 45, as said below
Outputs:
- grad_queries: bfloat16 [4, 3072, 1024], P('fsdp', 'ctx')
- grad_keys: bfloat16 [4, 3072, 1024], P('fsdp', 'ctx')
- grad_values: bfloat16 [4, 3072, 1024], P('fsdp', 'ctx')
- grad_out_weight: float32 [1024, 2048], P('fsdp', 'ctx')
Inputs may be any that keep to these rules, and one draw needn't show every extreme that they name: `patch_index`: along each folio the numbers rise strictly, by 1 to 3 from one token to the next except before the last token, start at 0 and end at 9213. `pair_lists`: the first pair_counts entries of a device's list are distinct pairs (q, w) with q < 3 and w < 15, in no particular order; every device lists the 3 pairs (q, 6 + q). Entries from the count on are arbitrary pairs of the same ranges and are not attended. `pair_counts`: in every folio some device lists all 45 pairs.
All inputs are finite; a program needn't handle non-finite values.
Results may differ from a plain program's by a relative error of at most 0.015.
Values may be sent and summed in bfloat16 or wider, within the bound.
A program may use at most 192 MiB of HBM per device.

v0:
```python
import math

import jax
import jax.numpy as jnp
from jax import lax
from jax.sharding import PartitionSpec as P

BLOCK = 128
REACH = 2
GRID = 1024


masked_fill = -1e30


def passed_along(block, axis, distance):
    devices = range(lax.axis_size(axis))
    route = [((i - distance) % len(devices), i) for i in devices]
    return lax.ppermute(block, axis, route)


def head_scores(query_heads, key_heads, distance, token_mask, slopes):
    scaling = 1.0 / math.sqrt(query_heads.shape[2])
    logits = (
        jnp.einsum("qhd,khd->hqk", query_heads, key_heads, preferred_element_type=jnp.float32)
        * scaling
    )
    logits = logits - slopes[:, None, None] * distance[None]
    return jnp.where(token_mask[None], logits, masked_fill)


def pair_distance(query_pos, key_pos):
    row_gap = jnp.abs(query_pos[:, None] // GRID - key_pos[None, :] // GRID)
    column_gap = jnp.abs(query_pos[:, None] % GRID - key_pos[None, :] % GRID)
    return (row_gap + column_gap).astype(jnp.float32)


def stats_update(running, query_heads, key_heads, value_heads, distance, token_mask, slopes):
    row_top, row_total, weighted = running
    logits = head_scores(query_heads, key_heads, distance, token_mask, slopes)
    new_top = jnp.maximum(row_top, jnp.max(logits, axis=2))
    factor = jnp.exp(row_top - new_top)
    exp_terms = jnp.where(token_mask[None], jnp.exp(logits - new_top[:, :, None]), 0.0)
    row_total = row_total * factor + jnp.sum(exp_terms, axis=2)
    weighted = weighted * factor.T[:, :, None] + jnp.einsum(
        "hqk,khd->qhd",
        exp_terms.astype(jnp.bfloat16),
        value_heads,
        preferred_element_type=jnp.float32,
    )
    return (new_top, row_total, weighted)


def grads_update(
    query_grad,
    query_heads,
    key_heads,
    value_heads,
    distance,
    token_mask,
    slopes,
    row_top,
    row_total,
    out_grad,
    row_delta,
):
    scaling = 1.0 / math.sqrt(query_heads.shape[2])
    logits = head_scores(query_heads, key_heads, distance, token_mask, slopes)
    prob_values = jnp.where(
        token_mask[None], jnp.exp(logits - row_top[:, :, None]) / row_total[:, :, None], 0.0
    )
    prob_grad = jnp.einsum(
        "qhd,khd->hqk", out_grad, value_heads, preferred_element_type=jnp.float32
    )
    score_grad = (prob_values * (prob_grad - row_delta[:, :, None])).astype(jnp.bfloat16)
    query_grad = query_grad + jnp.einsum(
        "hqk,khd->qhd", score_grad, key_heads, preferred_element_type=jnp.float32
    )
    key_part = (
        jnp.einsum("hqk,qhd->khd", score_grad, query_heads, preferred_element_type=jnp.float32)
        * scaling
    )
    value_part = jnp.einsum(
        "hqk,qhd->khd",
        prob_values.astype(jnp.bfloat16),
        out_grad,
        preferred_element_type=jnp.float32,
    )
    return (query_grad, key_part, value_part)


def window_blocks(key_values):
    visits = {}
    visits[0] = key_values
    above_side = key_values
    below_side = key_values
    for offset in range(1, REACH + 1):
        above_side = passed_along(above_side, "ctx", -1)
        below_side = passed_along(below_side, "ctx", 1)
        visits[offset] = above_side
        visits[-offset] = below_side
    return visits


def on_device(
    queries, keys, values, upstream, out_weight, slopes, patch_index, pair_lists, pair_counts
):
    loop_size = lax.axis_size("ctx")
    self_index = lax.axis_index("ctx")
    token_count = queries.shape[1]
    inner_width = queries.shape[2]
    head_count = slopes.shape[0]
    head_size = inner_width // head_count
    block_count = token_count // BLOCK
    slot_count = (2 * REACH + 1) * block_count
    scaling = 1.0 / math.sqrt(head_size)

    def expand_mask(block_columns):
        return jnp.broadcast_to(
            block_columns[:, None, :, None],
            (block_columns.shape[0], BLOCK, block_columns.shape[1], BLOCK),
        ).reshape(block_columns.shape[0] * BLOCK, block_columns.shape[1] * BLOCK)

    query_heads = queries[0].reshape(token_count, head_count, head_size)
    key_values = jnp.stack([keys[0], values[0]])
    upstream_rows = upstream[0]
    positions = patch_index[0]
    query_pos = lax.dynamic_slice_in_dim(positions, self_index * token_count, token_count)
    pair_rows = pair_lists[0]
    listed = (jnp.arange(pair_rows.shape[1]) < pair_counts[0, 0]).astype(jnp.float32)
    query_onehot = (pair_rows[0][:, None] == jnp.arange(block_count)[None, :]).astype(
        jnp.float32
    ) * listed[:, None]
    slot_onehot = (pair_rows[1][:, None] == jnp.arange(slot_count)[None, :]).astype(jnp.float32)
    block_mask = jnp.dot(query_onehot.T, slot_onehot, preferred_element_type=jnp.float32) > 0.5
    visits = window_blocks(key_values)
    visit_data = []
    for offset in range(-REACH, REACH + 1):
        arrived = visits[offset]
        key_heads = arrived[0].reshape(token_count, head_count, head_size)
        value_heads = arrived[1].reshape(token_count, head_count, head_size)
        key_pos = lax.dynamic_slice_in_dim(
            positions, (self_index + offset) % loop_size * token_count, token_count
        )
        distance = pair_distance(query_pos, key_pos)
        block_columns = block_mask[
            :, (offset + REACH) * block_count : (offset + REACH + 1) * block_count
        ]
        visit_data.append((offset, key_heads, value_heads, distance, block_columns))
    running = (
        jnp.full((head_count, token_count), masked_fill, jnp.float32),
        jnp.zeros((head_count, token_count), jnp.float32),
        jnp.zeros((token_count, head_count, head_size), jnp.float32),
    )
    for offset, key_heads, value_heads, distance, block_columns in visit_data:
        running = stats_update(
            running,
            query_heads,
            key_heads,
            value_heads,
            distance,
            expand_mask(block_columns),
            slopes,
        )
    row_top, row_total, weighted = running
    attended = (
        (weighted / row_total.T[:, :, None]).reshape(token_count, inner_width).astype(jnp.bfloat16)
    )
    out_grad_rows = lax.dot_general(
        upstream_rows,
        lax.all_gather(out_weight, "fsdp", axis=0, tiled=True),
        (((1,), (1,)), ((), ())),
        preferred_element_type=jnp.float32,
    ).astype(jnp.bfloat16)
    out_grad = out_grad_rows.reshape(token_count, head_count, head_size)
    row_delta = jnp.sum(
        out_grad.astype(jnp.float32)
        * attended.reshape(token_count, head_count, head_size).astype(jnp.float32),
        axis=2,
    ).T
    query_grad = jnp.zeros((token_count, head_count, head_size), jnp.float32)
    home_sums = jnp.zeros((2, token_count, inner_width), jnp.float32)
    for offset, key_heads, value_heads, distance, block_columns in visit_data:
        query_grad, key_part, value_part = grads_update(
            query_grad,
            query_heads,
            key_heads,
            value_heads,
            distance,
            expand_mask(block_columns),
            slopes,
            row_top,
            row_total,
            out_grad,
            row_delta,
        )
        partial_grads = (
            jnp.stack([key_part, value_part])
            .reshape(2, token_count, inner_width)
            .astype(jnp.bfloat16)
        )
        if offset == 0:
            home_sums = home_sums + partial_grads.astype(jnp.float32)
        else:
            home_sums = home_sums + passed_along(partial_grads, "ctx", offset).astype(jnp.float32)
    grad_queries = (query_grad * scaling).reshape(token_count, inner_width).astype(jnp.bfloat16)
    grad_keys = home_sums[0].astype(jnp.bfloat16)
    grad_values = home_sums[1].astype(jnp.bfloat16)
    total_tokens = token_count * loop_size * lax.axis_size("fsdp")
    grouped = lax.psum_scatter(
        lax.dot_general(
            attended, upstream_rows, (((0,), (0,)), ((), ())), preferred_element_type=jnp.float32
        ).astype(jnp.bfloat16),
        "fsdp",
        scatter_dimension=0,
        tiled=True,
    )
    weight_grad = lax.psum_scatter(grouped, "ctx", scatter_dimension=1, tiled=True).astype(
        jnp.float32
    )
    weight_grad = weight_grad / math.sqrt(total_tokens)
    return (grad_queries[None], grad_keys[None], grad_values[None], weight_grad)


def solution(mesh):
    in_specs = (
        P("fsdp", "ctx", None),
        P("fsdp", "ctx", None),
        P("fsdp", "ctx", None),
        P("fsdp", "ctx", None),
        P("fsdp", None),
        P(),
        P("fsdp", None),
        P("fsdp", None, "ctx"),
        P("fsdp", "ctx"),
    )
    out_specs = (
        P("fsdp", "ctx", None),
        P("fsdp", "ctx", None),
        P("fsdp", "ctx", None),
        P("fsdp", "ctx"),
    )
    return jax.shard_map(
        on_device, mesh=mesh, in_specs=in_specs, out_specs=out_specs, check_vma=False
    )
```

profile of v0, /device:TPU:0, one launch (start us, length us, event | category | flops | bytes accessed | tf_op | source)
XLA Modules:
  0.0 372.6 jit_solution(6831137021879583989)
XLA Ops:
  13.6 3.0 collective-permute-start
  16.5 3.0 collective-permute-start.2
  25.4 4.2 %broadcast_multiply_fusion = f32[8,384,384]{2,1,0:T(8,128)} fusion(bf16[384,8,128]{0,2,1:T(8,128)(2,1)} %bitcast.304, bf16[384,8,128]{0,2,1:T(8,128)(2,1)S(1)} %bitcast.302), kind=kOutput, calls=%fused_computation.61 | convolution fusion | flops 303169536 | bytes 6291456 | tf_op jit(solution)/shard_map/qhd,khd->hqk/dot_general | solution.py:25
  29.6 6.1 %copy.104 = f32[8,384,384]{1,2,0:T(8,128)} copy(f32[8,384,384]{2,1,0:T(8,128)} %broadcast_multiply_fusion) | data formatting | bytes 9437184 | tf_op jit(solution)/shard_map/mul | solution.py:25
  40.8 43.4 %collective-permute-done = bf16[2,384,1024]{1,2,0:T(8,128)(2,1)} collective-permute-done((bf16[2,384,1024]{1,2,0:T(8,128)(2,1)}, bf16[2,384,1024]{1,2,0:T(8,128)(2,1)}, u32[]{:S(2)}, u32[]{:S(2)}) %collective-permute-start) | collective-permute-done | bytes 1572896 | tf_op jit(solution)/shard_map/ppermute | solution.py:19
  86.7 3.1 fusion.113
  89.8 3.6 collective-permute-start.3
  96.6 3.6 fusion.120
  101.8 51.7 %collective-permute-done.1 = bf16[2,384,1024]{1,2,0:T(8,128)(2,1)S(1)} collective-permute-done((bf16[2,384,1024]{1,2,0:T(8,128)(2,1)}, bf16[2,384,1024]{1,2,0:T(8,128)(2,1)S(1)}, u32[]{:S(2)}, u32[]{:S(2)}) %collective-permute-start.1) | collective-permute-done | bytes 1572896 | tf_op jit(solution)/shard_map/ppermute | solution.py:19
  154.6 2.6 collective-permute-done.3
  175.1 3.1 fusion.14
  178.2 4.9 %fusion.57 = bf16[384,1024]{1,0:T(8,128)(2,1)} fusion(bf16[1024,2048]{1,0:T(8,128)(2,1)} %all-gather.2.cloned.1.call-done, bf16[1,384,2048]{2,1,0:T(8,128)(2,1)S(1)} %copy-done), kind=kOutput, calls=%fused_computation.97 | convolution fusion | flops 1611005952 | bytes 6553600 | tf_op jit(solution)/shard_map/dot_general | solution.py:169
  185.4 4.7 %fusion.60 = bf16[8,128,384]{2,1,0:T(8,128)(2,1)} fusion(bf16[384,8,128]{0,2,1:T(8,128)(2,1)} %bitcast.332, f32[8,384,384]{1,2,0:T(8,128)} %copy-done.3, f32[8,384]{1,0:T(8,128)S(1)} %multiply_add_fusion, f32[8,384]{1,0:T(8,128)S(1)} %get-tuple-element.27, pred[384,384]{0,1:T(8,128)(4,1)} %copy-done.31), kind=kOutput, calls=%fused_computation.98 | convolution fusion | flops 307101696 | bytes 6463488 | tf_op jit(solution)/shard_map/hqk,qhd->khd/dot_general | solution.py:83
  194.5 7.3 %multiply_reduce_fusion = (f32[384,8]{0,1:T(8,128)S(1)}, bf16[384,8,128]{0,2,1:T(8,128)(2,1)}) fusion(bf16[384,1024]{0,1:T(8,128)(2,1)} %copy.206, f32[384,8]{0,1:T(8,128)S(1)} %get-tuple-element.23, bf16[384,8,128]{0,2,1:T(8,128)(2,1)} %bitcast.357, f32[8,384,384]{1,2,0:T(8,128)} %copy-done.6, f32[8,384]{1,0:T(8,128)S(1)} %get-tuple-element.27, ...), kind=kOutput, calls=%fused_computation.96 | convolution fusion | flops 311424000 | bytes 13615104 | tf_op jit(solution)/shard_map/hqk,khd->qhd/dot_general | solution.py:45
  208.1 2.7 pad_maximum_fusion.1
  214.1 5.5 %convolution_convert_fusion = bf16[1024,2048]{1,0:T(8,128)(2,1)} fusion(bf16[384,1024]{0,1:T(8,128)(2,1)} %bitcast.364, bf16[1,384,2048]{2,1,0:T(8,128)(2,1)S(1)} %copy-done), kind=kOutput, calls=%fused_computation.34 | convolution fusion | flops 1612709888 | bytes 6553600 | tf_op jit(solution)/shard_map/dot_general | solution.py:211
  219.7 4.5 %multiply_convert_fusion.3 = bf16[8,384,384]{1,2,0:T(8,128)(2,1)S(1)} fusion(f32[8,384]{1,0:T(8,128)S(1)} %bitcast.366, bf16[384,8,128]{0,2,1:T(8,128)(2,1)} %bitcast.333, bf16[384,8,128]{0,2,1:T(8,128)(2,1)} %bitcast.326, f32[8,384]{1,0:T(8,128)S(1)} %multiply_add_fusion, f32[8,384,384]{1,2,0:T(8,128)} %copy-done.4, f32[8,384]{1,0:T(8,128)S(1)} %get-tuple-element.27, ...), kind=kOutput, calls=%fused_computation.14 | convolution fusion | flops 309067776 | bytes 8835072 | tf_op jit(solution)/shard_map/qhd,khd->hqk/dot_general | solution.py:72
  234.5 4.5 %fusion.69 = bf16[8,128,384]{2,1,0:T(8,128)(2,1)} fusion(bf16[384,8,128]{0,2,1:T(8,128)(2,1)} %bitcast.334, f32[8,384,384]{1,2,0:T(8,128)} %copy-done.2, f32[8,384]{1,0:T(8,128)S(1)} %multiply_add_fusion, f32[8,384]{1,0:T(8,128)S(1)} %get-tuple-element.27, pred[384,384]{0,1:T(8,128)(4,1)S(1)} %copy-done.30), kind=kOutput, calls=%fused_computation.101 | convolution fusion | flops 307101696 | bytes 6463488 | tf_op jit(solution)/shard_map/hqk,qhd->khd/dot_general | solution.py:83
  240.5 4.4 %multiply_convert_fusion.1 = bf16[8,384,384]{1,2,0:T(8,128)(2,1)S(1)} fusion(f32[8,384]{1,0:T(8,128)S(1)} %bitcast.367, bf16[384,8,128]{0,2,1:T(8,128)(2,1)} %bitcast.335, bf16[384,8,128]{0,2,1:T(8,128)(2,1)} %bitcast.325, f32[8,384]{1,0:T(8,128)S(1)} %multiply_add_fusion, f32[8,384,384]{1,2,0:T(8,128)} %copy-done.2, f32[8,384]{1,0:T(8,128)S(1)} %get-tuple-element.27, ...), kind=kOutput, calls=%fused_computation.10 | convolution fusion | flops 309067776 | bytes 8835072 | tf_op jit(solution)/shard_map/qhd,khd->hqk/dot_general | solution.py:72
  253.1 4.5 %fusion.72 = bf16[8,128,384]{2,1,0:T(8,128)(2,1)} fusion(bf16[384,8,128]{0,2,1:T(8,128)(2,1)} %bitcast.336, f32[8,384,384]{1,2,0:T(8,128)} %copy-done.6, f32[8,384]{1,0:T(8,128)S(1)} %multiply_add_fusion, f32[8,384]{1,0:T(8,128)S(1)} %get-tuple-element.27, pred[384,384]{0,1:T(8,128)(4,1)S(1)} %copy-done.45), kind=kOutput, calls=%fused_computation.102 | convolution fusion | flops 307101696 | bytes 6463488 | tf_op jit(solution)/shard_map/hqk,qhd->khd/dot_general | solution.py:83
  259.1 4.4 %multiply_convert_fusion = bf16[8,384,384]{1,2,0:T(8,128)(2,1)S(1)} fusion(f32[8,384]{1,0:T(8,128)S(1)} %bitcast.368, bf16[384,8,128]{0,2,1:T(8,128)(2,1)} %bitcast.337, bf16[384,8,128]{0,2,1:T(8,128)(2,1)} %bitcast.358, f32[8,384]{1,0:T(8,128)S(1)} %multiply_add_fusion, f32[8,384,384]{1,2,0:T(8,128)} %copy-done.6, f32[8,384]{1,0:T(8,128)S(1)} %get-tuple-element.27, ...), kind=kOutput, calls=%fused_computation.8 | convolution fusion | flops 309067776 | bytes 8835072 | tf_op jit(solution)/shard_map/qhd,khd->hqk/dot_general | solution.py:72
  269.4 2.6 fusion.128
  272.1 2.8 fusion.66
  274.8 3.2 multiply_convert_fusion.2
  279.9 3.6 multiply_convert_fusion.7
  288.1 2.5 fusion.130
  290.6 2.6 fusion.129
  297.4 6.1 %collective-permute-done.5 = bf16[2,384,1024]{2,1,0:T(8,128)(2,1)} collective-permute-done((bf16[2,384,1024]{2,1,0:T(8,128)(2,1)}, bf16[2,384,1024]{2,1,0:T(8,128)(2,1)}, u32[]{:S(2)}, u32[]{:S(2)}) %collective-permute-start.5) | collective-permute-done | bytes 1572896 | tf_op jit(solution)/shard_map/ppermute | solution.py:19
  303.5 13.1 %collective-permute-done.6 = bf16[2,384,1024]{2,1,0:T(8,128)(2,1)} collective-permute-done((bf16[2,384,1024]{2,1,0:T(8,128)(2,1)}, bf16[2,384,1024]{2,1,0:T(8,128)(2,1)}, u32[]{:S(2)}, u32[]{:S(2)}) %collective-permute-start.6) | collective-permute-done | bytes 1572896 | tf_op jit(solution)/shard_map/ppermute | solution.py:19
  316.6 5.9 %collective-permute-done.7 = bf16[2,384,1024]{2,1,0:T(8,128)(2,1)} collective-permute-done((bf16[2,384,1024]{2,1,0:T(8,128)(2,1)}, bf16[2,384,1024]{2,1,0:T(8,128)(2,1)}, u32[]{:S(2)}, u32[]{:S(2)}) %collective-permute-start.7) | collective-permute-done | bytes 1572896 | tf_op jit(solution)/shard_map/ppermute | solution.py:19
  322.5 4.7 %add_convert_fusion = bf16[2,384,1024]{2,1,0:T(8,128)(2,1)S(1)} fusion(bf16[2,384,1024]{2,1,0:T(8,128)(2,1)} %collective-permute-done.7, bf16[2,384,1024]{2,1,0:T(8,128)(2,1)} %collective-permute-done.6, bf16[2,384,1024]{2,1,0:T(8,128)(2,1)} %collective-permute-done.5, bf16[2,384,1024]{2,1,0:T(8,128)(2,1)} %collective-permute-done.4, ...), kind=kLoop, calls=%fused_computation.35 | loop fusion | flops 8650752 | bytes 9437184 | tf_op jit(solution)/shard_map/convert.1
  328.5 35.7 %reduce-scatter.5.cloned.1.call-done = bf16[256,256]{1,0:T(8,128)(2,1)} async-done(((bf16[256,2048]{1,0:T(8,128)(2,1)}), bf16[256,256]{1,0:T(8,128)(2,1)}) %reduce-scatter.5.cloned.1.call-update) | async-done | bytes 131088 | tf_op jit(solution)/shard_map/reduce_scatter | solution.py:218
  (206 shorter events, 99.7 us)
Async XLA Ops:
  7.2 171.0 %copy-start = (bf16[1,384,2048]{2,1,0:T(8,128)(2,1)S(1)}, bf16[1,384,2048]{2,1,0:T(8,128)(2,1)}, u32[]{:S(2)}) copy-start(bf16[1,384,2048]{2,1,0:T(8,128)(2,1)} %param.12) | copy-start | bytes 4718596
  7.2 12.5 %copy-start.48 = (s32[1,2,45]{2,1,0:T(2,128)S(1)}, s32[1,2,45]{2,1,0:T(2,128)}, u32[]{:S(2)}) copy-start(s32[1,2,45]{2,1,0:T(2,128)} %param.16) | copy-start | bytes 1084
  7.2 171.0 %all-gather.2.cloned.1.call-start = ((), (), s32[]{:S(2)}) async-start(), calls=%async_computation.2 | async-start | bytes 5242880 | tf_op jit(solution)/shard_map/all_gather | solution.py:171
  13.6 70.6 %collective-permute-start = (bf16[2,384,1024]{1,2,0:T(8,128)(2,1)}, bf16[2,384,1024]{1,2,0:T(8,128)(2,1)}, u32[]{:S(2)}, u32[]{:S(2)}) collective-permute-start(bf16[2,384,1024]{1,2,0:T(8,128)(2,1)} %pad_maximum_fusion), channel_id=1, source_target_pairs={{28,0},{0,4},{4,8},{8,12},{12,16},{16,20},{20,24},{24,28},{29,1},{... | collective-permute-start | bytes 4718600 | tf_op jit(solution)/shard_map/ppermute | solution.py:19
  16.5 73.2 %collective-permute-start.2 = (bf16[2,384,1024]{1,2,0:T(8,128)(2,1)}, bf16[2,384,1024]{1,2,0:T(8,128)(2,1)}, u32[]{:S(2)}, u32[]{:S(2)}) collective-permute-start(bf16[2,384,1024]{1,2,0:T(8,128)(2,1)} %pad_maximum_fusion), channel_id=1, source_target_pairs={{4,0},{8,4},{12,8},{16,12},{20,16},{24,20},{28,24},{0,28},{5,1},{9... | collective-permute-start | bytes 4718600 | tf_op jit(solution)/shard_map/ppermute | solution.py:19
  19.6 260.3 %reduce-scatter.3.cloned.1.call-start = ((), (), s32[]{:S(2)}) async-start(), calls=%async_computation.3 | async-start | bytes 5242880 | tf_op jit(solution)/shard_map/reduce_scatter | solution.py:210
  21.3 147.3 %copy-start.31 = (pred[384,384]{0,1:T(8,128)(4,1)}, pred[384,384]{0,1:T(8,128)(4,1)S(1)}, u32[]{:S(2)}) copy-start(pred[384,384]{0,1:T(8,128)(4,1)S(1)} %copy.94) | copy-start | bytes 442372
  24.2 148.7 %copy-start.29 = (pred[384,384]{0,1:T(8,128)(4,1)}, pred[384,384]{0,1:T(8,128)(4,1)S(1)}, u32[]{:S(2)}) copy-start(pred[384,384]{0,1:T(8,128)(4,1)S(1)} %copy.105) | copy-start | bytes 442372
  29.6 10.0 %copy-start.46 = (s32[1,3072]{1,0:T(1,128)S(1)}, s32[1,3072]{1,0:T(1,128)}, u32[]{:S(2)}) copy-start(s32[1,3072]{1,0:T(1,128)} %param.15) | copy-start | bytes 36868
  35.7 51.0 %copy-start.47 = (f32[8]{0:T(128)S(1)}, f32[8]{0:T(128)}, u32[]{:S(2)}) copy-start(f32[8]{0:T(128)} %param.14) | copy-start | bytes 100
  36.2 138.8 %copy-start.33 = (pred[384,384]{0,1:T(8,128)(4,1)}, pred[384,384]{0,1:T(8,128)(4,1)S(1)}, u32[]{:S(2)}) copy-start(pred[384,384]{0,1:T(8,128)(4,1)S(1)} %copy.100) | copy-start | bytes 442372
  40.8 54.1 %copy-start.7 = (bf16[1,384,1024]{1,2,0:T(8,128)(2,1)S(1)}, bf16[1,384,1024]{1,2,0:T(8,128)(2,1)}, u32[]{:S(2)}) copy-start(bf16[1,384,1024]{1,2,0:T(8,128)(2,1)} %copy.204) | copy-start | bytes 2359300
  84.2 69.3 %collective-permute-start.1 = (bf16[2,384,1024]{1,2,0:T(8,128)(2,1)}, bf16[2,384,1024]{1,2,0:T(8,128)(2,1)S(1)}, u32[]{:S(2)}, u32[]{:S(2)}) collective-permute-start(bf16[2,384,1024]{1,2,0:T(8,128)(2,1)} %collective-permute-done), channel_id=1, source_target_pairs={{28,0},{0,4},{4,8},{8,12},{12,16},{16,20},{20,24},{24,28},{29,1},{... | collective-permute-start | bytes 4718600 | tf_op jit(solution)/shard_map/ppermute | solution.py:19
  89.8 67.4 %collective-permute-start.3 = (bf16[2,384,1024]{1,2,0:T(8,128)(2,1)}, bf16[2,384,1024]{1,2,0:T(8,128)(2,1)S(1)}, u32[]{:S(2)}, u32[]{:S(2)}) collective-permute-start(bf16[2,384,1024]{1,2,0:T(8,128)(2,1)} %collective-permute-done.2), channel_id=1, source_target_pairs={{4,0},{8,4},{12,8},{16,12},{20,16},{24,20},{28,24},{0,28},{5,1},{9... | collective-permute-start | bytes 4718600 | tf_op jit(solution)/shard_map/ppermute | solution.py:19
  94.9 78.0 %copy-start.19 = (bf16[1,384,1024]{1,2,0:T(8,128)(2,1)}, bf16[1,384,1024]{1,2,0:T(8,128)(2,1)S(1)}, u32[]{:S(2)}) copy-start(bf16[1,384,1024]{1,2,0:T(8,128)(2,1)S(1)} %get-tuple-element.39) | copy-start | bytes 2359300
  96.6 76.3 %copy-start.2 = (f32[8,384,384]{1,2,0:T(8,128)}, f32[8,384,384]{1,2,0:T(8,128)S(1)}, u32[]{:S(2)}) copy-start(f32[8,384,384]{1,2,0:T(8,128)S(1)} %get-tuple-element.66) | copy-start | bytes 14155780
  101.8 68.9 %copy-start.4 = (f32[8,384,384]{1,2,0:T(8,128)}, f32[8,384,384]{1,2,0:T(8,128)S(1)}, u32[]{:S(2)}) copy-start(f32[8,384,384]{1,2,0:T(8,128)S(1)} %get-tuple-element.68) | copy-start | bytes 14155780
  159.9 8.7 %copy-start.3 = (f32[8,384,384]{1,2,0:T(8,128)}, f32[8,384,384]{1,2,0:T(8,128)S(1)}, u32[]{:S(2)}) copy-start(f32[8,384,384]{1,2,0:T(8,128)S(1)} %get-tuple-element.70) | copy-start | bytes 14155780
  192.1 9.7 %slice-start.4 = ((s8[4718592]{0:T(1024)(128)(4,1)}), s8[524288]{0:T(1024)(128)(4,1)S(1)}, s32[]{:S(2)}) async-start(s8[4718592]{0:T(1024)(128)(4,1)} %bitcast.298), calls=%async_computation.9 | async-start | bytes 1048576
  194.5 7.3 %slice-start.5 = ((s8[4718592]{0:T(1024)(128)(4,1)}), s8[4194304]{0:T(1024)(128)(4,1)S(1)}, s32[]{:S(2)}) async-start(s8[4718592]{0:T(1024)(128)(4,1)} %bitcast.298), calls=%async_computation.10 | async-start | bytes 8388608
  194.5 7.3 %copy-start.22 = (bf16[1,384,1024]{1,2,0:T(8,128)(2,1)S(1)}, bf16[1,384,1024]{1,2,0:T(8,128)(2,1)}, u32[]{:S(2)}) copy-start(bf16[1,384,1024]{1,2,0:T(8,128)(2,1)} %get-tuple-element.35) | copy-start | bytes 2359300
  194.5 7.3 %copy-start.32 = (pred[384,384]{0,1:T(8,128)(4,1)S(1)}, pred[384,384]{0,1:T(8,128)(4,1)}, u32[]{:S(2)}) copy-start(pred[384,384]{0,1:T(8,128)(4,1)} %copy-done.31) | copy-start | bytes 442372
  194.5 7.4 %copy-start.41 = (bf16[384,1024]{0,1:T(8,128)(2,1)S(1)}, bf16[384,1024]{0,1:T(8,128)(2,1)}, u32[]{:S(2)}) copy-start(bf16[384,1024]{0,1:T(8,128)(2,1)} %copy.206) | copy-start | bytes 2359300
  210.7 86.7 %collective-permute-start.4 = (bf16[2,384,1024]{2,1,0:T(8,128)(2,1)}, bf16[2,384,1024]{2,1,0:T(8,128)(2,1)}, u32[]{:S(2)}, u32[]{:S(2)}) collective-permute-start(bf16[2,384,1024]{2,1,0:T(8,128)(2,1)} %pad_maximum_fusion.1), channel_id=1, source_target_pairs={{8,0},{12,4},{16,8},{20,12},{24,16},{28,20},{0,24},{4,28},{9,1},{1... | collective-permute-start | bytes 4718600 | tf_op jit(solution)/shard_map/ppermute | solution.py:19
  219.7 144.5 %reduce-scatter.5.cloned.1.call-start = ((), (), s32[]{:S(2)}) async-start(), calls=%async_computation.4 | async-start | bytes 1179648 | tf_op jit(solution)/shard_map/reduce_scatter | solution.py:218
  225.6 8.9 %copy-start.30 = (pred[384,384]{0,1:T(8,128)(4,1)S(1)}, pred[384,384]{0,1:T(8,128)(4,1)}, u32[]{:S(2)}) copy-start(pred[384,384]{0,1:T(8,128)(4,1)} %copy-done.29) | copy-start | bytes 442372
  232.3 71.3 %collective-permute-start.5 = (bf16[2,384,1024]{2,1,0:T(8,128)(2,1)}, bf16[2,384,1024]{2,1,0:T(8,128)(2,1)}, u32[]{:S(2)}, u32[]{:S(2)}) collective-permute-start(bf16[2,384,1024]{2,1,0:T(8,128)(2,1)} %pad_maximum_fusion.2), channel_id=1, source_target_pairs={{4,0},{8,4},{12,8},{16,12},{20,16},{24,20},{28,24},{0,28},{5,1},{9... | collective-permute-start | bytes 4718600 | tf_op jit(solution)/shard_map/ppermute | solution.py:19
  252.8 63.7 %collective-permute-start.6 = (bf16[2,384,1024]{2,1,0:T(8,128)(2,1)}, bf16[2,384,1024]{2,1,0:T(8,128)(2,1)}, u32[]{:S(2)}, u32[]{:S(2)}) collective-permute-start(bf16[2,384,1024]{2,1,0:T(8,128)(2,1)} %pad_maximum_fusion.3), channel_id=1, source_target_pairs={{28,0},{0,4},{4,8},{8,12},{12,16},{16,20},{20,24},{24,28},{29,1},{... | collective-permute-start | bytes 4718600 | tf_op jit(solution)/shard_map/ppermute | solution.py:19
  268.1 54.4 %collective-permute-start.7 = (bf16[2,384,1024]{2,1,0:T(8,128)(2,1)}, bf16[2,384,1024]{2,1,0:T(8,128)(2,1)}, u32[]{:S(2)}, u32[]{:S(2)}) collective-permute-start(bf16[2,384,1024]{2,1,0:T(8,128)(2,1)} %pad_maximum_fusion.4), channel_id=1, source_target_pairs={{24,0},{28,4},{0,8},{4,12},{8,16},{12,20},{16,24},{20,28},{25,1},{... | collective-permute-start | bytes 4718600 | tf_op jit(solution)/shard_map/ppermute | solution.py:19
  293.3 29.2 %copy-start.10 = (bf16[1,384,1024]{2,1,0:T(8,128)(2,1)S(1)}, bf16[1,384,1024]{2,1,0:T(8,128)(2,1)}, u32[]{:S(2)}) copy-start(bf16[1,384,1024]{2,1,0:T(8,128)(2,1)} %copy.156) | copy-start | bytes 2359300
  293.3 29.2 %copy-start.11 = (bf16[1,384,1024]{2,1,0:T(8,128)(2,1)S(1)}, bf16[1,384,1024]{2,1,0:T(8,128)(2,1)}, u32[]{:S(2)}) copy-start(bf16[1,384,1024]{2,1,0:T(8,128)(2,1)} %copy.155) | copy-start | bytes 2359300
  295.0 70.8 %copy-start.1 = (bf16[1,384,2048]{2,1,0:T(8,128)(2,1)S(1)}, bf16[1,384,2048]{2,1,0:T(8,128)(2,1)}, u32[]{:S(2)}) copy-start(bf16[1,384,2048]{2,1,0:T(8,128)(2,1)} %param.12) | copy-start | bytes 4718596
  (38 other events, 149.0 us)
Sparse Core Ops, SparseCore 0:
  19.7 33.2 all-gather.1
  219.8 43.5 reduce-scatter.2
  280.1 84.0 reduce-scatter.4
where the time goes:
time: 379 us; the launch traced here: 373 us
  waiting for transfers between devices  159 us (42%)
  matrix products  97.4 us (26%)
  local copies, waits for them, and re-layouts  56.7 us (15%)
  other arithmetic  27.5 us (7%)
  starting transfers between devices  17.1 us (5%)
  between operations  15.3 us (4%)
    ppermute x8, waiting for transfers between devices, passed_along(): return lax.ppermute(block, axis, route)  123 us
    reduce_scatter x1, waiting for transfers between devices, on_device(): lax.psum_scatter(grouped, 'ctx', scatter_dimension=1, tiled=True)  35.7 us
    another operation x10, local copies, waits for them, and re-layouts, on_device(): jnp.stack([key_part, value_part]).reshape(2, token_count, inner_width)  20.6 us
    dot_general x5, matrix products, grads_update(): jnp.einsum('hqk,qhd->khd', prob_values.astype(jnp.bfloat16), out_grad, pr...  18.5 us
    dot_general x5, matrix products, grads_update(): jnp.einsum('qhd,khd->hqk', out_grad, value_heads, preferred_element_type=...  18.3 us
    ppermute x8, starting transfers between devices, passed_along(): return lax.ppermute(block, axis, route)  17 us
    dot_general x5, matrix products, stats_update(): jnp.einsum('hqk,khd->qhd', exp_terms.astype(jnp.bfloat16), value_heads, p...  16.9 us
    unnamed x127, local copies, waits for them, and re-layouts  13.2 us
  transfers between devices with their start and end apart: 11, of which 7 were waited for; matrix products, arithmetic and copies ran while one was open for 37% of the time, Pallas kernels for 0%

commit v1 on v0

v1 whole, which is shorter than its diff:
```python
import functools
import math

import jax
import jax.numpy as jnp
from jax import lax
from jax.experimental import pallas as pl
from jax.experimental.pallas import tpu as pltpu
from jax.sharding import PartitionSpec as P

BLOCK = 128
REACH = 2
GRID = 1024
FAR = 1e32
CHUNKS = 2
MESH = pl.DeviceIdType.MESH
F32 = jnp.float32
BF16 = jnp.bfloat16


def nt(a, b):
    return lax.dot_general(a, b, (((1,), (1,)), ((), ())), preferred_element_type=F32)


def nn(a, b):
    return lax.dot_general(a, b, (((1,), (0,)), ((), ())), preferred_element_type=F32)


def tn(a, b):
    return lax.dot_general(a, b, (((0,), (0,)), ((), ())), preferred_element_type=F32)


def greet(targets):
    barrier = pltpu.get_barrier_semaphore()
    for target in targets:
        pl.semaphore_signal(barrier, inc=1, device_id=target, device_id_type=MESH)
    pl.semaphore_wait(barrier, len(targets))


class Gather:
    def __init__(self, pieces, send_sem, recv_sem):
        n = lax.axis_size("ctx")
        me = lax.axis_index("ctx")
        self.parity = lax.rem(me, 2)
        self.up = lax.rem(me + 2, n)
        self.down = lax.rem(me + n - 2, n)
        self.partner = me + 1 - 2 * self.parity
        self.pieces = pieces
        self.send_sem = send_sem
        self.recv_sem = recv_sem

    def targets(self):
        return [{"ctx": self.up}, {"ctx": self.down}, {"ctx": self.partner}]

    def copy(self, i, slot):
        own, land = self.pieces[i]
        src = land(1 - self.parity) if slot == 3 else own
        target = (self.up, self.down, self.partner, self.partner)[slot]
        return pltpu.make_async_remote_copy(
            src_ref=src,
            dst_ref=land(slot),
            send_sem=self.send_sem.at[i, slot],
            recv_sem=self.recv_sem.at[i, slot],
            device_id={"ctx": target},
            device_id_type=MESH,
        )

    def start(self):
        for i in range(len(self.pieces)):
            for slot in (0, 1, 2):
                self.copy(i, slot).start()

    def relay(self, i):
        src = 1 - self.parity
        own, land = self.pieces[i]
        pltpu.make_async_remote_copy(
            src_ref=own,
            dst_ref=land(src),
            send_sem=self.send_sem.at[i, 0],
            recv_sem=self.recv_sem.at[i, src],
            device_id={"ctx": self.partner},
            device_id_type=MESH,
        ).wait_recv()
        self.copy(i, 3).start()

    def arrived(self, slot):
        for i in range(len(self.pieces)):
            own, land = self.pieces[i]
            pltpu.make_async_remote_copy(
                src_ref=own,
                dst_ref=land(slot),
                send_sem=self.send_sem.at[i, 0],
                recv_sem=self.recv_sem.at[i, slot],
                device_id={"ctx": self.partner},
                device_id_type=MESH,
            ).wait_recv()

    def sent(self):
        for i in range(len(self.pieces)):
            for slot in range(4):
                self.copy(i, slot).wait_send()


def row_pieces(own_ref, land_ref, index, chunks):
    rows = own_ref.shape[0] // chunks

    def piece(j):
        span = pl.ds(j * rows, rows)

        def land(slot):
            return land_ref.at[slot, index, span] if index is not None else land_ref.at[slot, span]

        return (own_ref.at[span], land)

    return [piece(j) for j in range(chunks)]


def build_distance(far_ref, wrow_ref, wcol_ref, key_at, query_at, mask_row, tokens):
    qs = pl.ds(pl.multiple_of(query_at * tokens, BLOCK), tokens)
    qr = wrow_ref[0:1, qs]
    qg = wrow_ref[1:2, qs]
    for b in range(tokens // BLOCK):
        ks = pl.ds(pl.multiple_of(key_at * tokens + b * BLOCK, BLOCK), BLOCK)
        kc = wcol_ref[ks, :]
        dist = jnp.abs(kc[:, 0:1] - qr) + jnp.abs(kc[:, 1:2] - qg)
        far_ref[b * BLOCK : (b + 1) * BLOCK, :] = jnp.where(mask_row(b) > 0.5, dist, FAR)


def head_span(h, size):
    return pl.ds(pl.multiple_of(h * size, size), size)


def forward_kernel(
    heads,
    slopes_ref,
    q_ref,
    k_ref,
    v_ref,
    up_ref,
    w_ref,
    wrow_ref,
    wcol_ref,
    mask_ref,
    kv_ref,
    og_ref,
    att_ref,
    stats_ref,
    wbuf_ref,
    far_ref,
    top_ref,
    total_ref,
    acc_ref,
    send_sem,
    recv_sem,
    wsend_sem,
    wrecv_sem,
):
    tokens, width = q_ref.shape
    size = width // heads
    blocks = tokens // BLOCK
    scaling = 1.0 / math.sqrt(size)
    nf = lax.axis_size("fsdp")
    fs = lax.axis_index("fsdp")
    wrows = w_ref.shape[0]
    gather = Gather(
        row_pieces(k_ref, kv_ref, 0, CHUNKS) + row_pieces(v_ref, kv_ref, 1, CHUNKS),
        send_sem,
        recv_sem,
    )
    greet(gather.targets() + [{"fsdp": lax.rem(fs + d, nf)} for d in range(1, nf)])
    gather.start()
    wcopies = [
        pltpu.make_async_remote_copy(
            src_ref=w_ref,
            dst_ref=wbuf_ref.at[d - 1],
            send_sem=wsend_sem.at[d - 1],
            recv_sem=wrecv_sem.at[d - 1],
            device_id={"fsdp": lax.rem(fs + d, nf)},
            device_id_type=MESH,
        )
        for d in range(1, nf)
    ]
    for copy in wcopies:
        copy.start()

    top_ref[...] = jnp.full(top_ref.shape, -1e30, F32)
    total_ref[...] = jnp.zeros(total_ref.shape, F32)
    acc_ref[...] = jnp.zeros(acc_ref.shape, F32)

    def visit(keys, values, offset):
        at = offset + REACH

        def mask_row(b):
            return mask_ref[pl.ds(at * blocks + b, 1), :]

        build_distance(far_ref, wrow_ref, wcol_ref, at, REACH, mask_row, tokens)

        @pl.loop(0, heads)
        def _(h):
            hs = head_span(h, size)
            s = nt(keys[:, hs], q_ref[:, hs]) * scaling - slopes_ref[h] * far_ref[...]
            old = top_ref[h]
            new = jnp.maximum(old, jnp.max(s, axis=0, keepdims=True))
            factor = jnp.exp(old - new)
            p = jnp.exp(s - new)
            top_ref[h] = new
            total_ref[h] = total_ref[h] * factor + jnp.sum(p, axis=0, keepdims=True)
            acc_ref[h] = acc_ref[h] * factor + tn(values[:, hs], p.astype(BF16))

    def visit_slot(slot, offset):
        visit(kv_ref.at[slot, 0], kv_ref.at[slot, 1], offset)

    def project(block, owner):
        cols = pl.ds(pl.multiple_of(owner * wrows, BLOCK), wrows)
        og_ref[:, cols] = nt(up_ref[...], block[...]).astype(BF16)

    parity = gather.parity
    near = 1 - 2 * parity
    visit(k_ref, v_ref, 0)
    project(w_ref, fs)
    for i in range(len(gather.pieces)):
        gather.relay(i)
    visit_slot(1 - parity, 2 * near)
    gather.arrived(2)
    visit_slot(2, near)
    for d in range(1, nf):
        wcopies[d - 1].wait()
        project(wbuf_ref.at[d - 1], lax.rem(fs + nf - d, nf))
    gather.arrived(parity)
    visit_slot(parity, -2 * near)
    gather.arrived(3)
    visit_slot(3, -near)
    for h in range(heads):
        hs = slice(h * size, (h + 1) * size)
        total = total_ref[h]
        att_t = acc_ref[h] / total
        att = att_t.T.astype(BF16)
        att_ref[:, hs] = att
        stats_ref[h : h + 1, :] = top_ref[h] + jnp.log(total)
        prod = og_ref[:, hs].astype(F32) * att.astype(F32)
        stats_ref[heads + h : heads + h + 1, :] = jnp.sum(prod.T, axis=0, keepdims=True)
    stats_ref[2 * heads :, :] = mask_ref[...]
    gather.sent()


def backward_kernel(
    heads,
    slopes_ref,
    q_ref,
    k_ref,
    v_ref,
    og_ref,
    stats_ref,
    kv_ref,
    wrow_ref,
    wcol_ref,
    dq_ref,
    dk_ref,
    dv_ref,
    qbuf_ref,
    obuf_ref,
    sbuf_ref,
    far_ref,
    dqt_ref,
    dka_ref,
    dva_ref,
    send_sem,
    recv_sem,
):
    tokens, width = q_ref.shape
    size = width // heads
    blocks = tokens // BLOCK
    scaling = 1.0 / math.sqrt(size)
    gather = Gather(
        row_pieces(stats_ref, sbuf_ref, None, 1)
        + row_pieces(q_ref, qbuf_ref, None, CHUNKS)
        + row_pieces(og_ref, obuf_ref, None, CHUNKS),
        send_sem,
        recv_sem,
    )
    greet(gather.targets())
    gather.start()

    def visit(keys, values, queries, grads, stats, key_at, query_at, to_query, to_key, first):
        def mask_row(b):
            return stats[pl.ds(2 * heads + (key_at - query_at + REACH) * blocks + b, 1), :]

        build_distance(far_ref, wrow_ref, wcol_ref, key_at, query_at, mask_row, tokens)

        @pl.loop(0, heads)
        def _(h):
            hs = head_span(h, size)
            k, q, g = keys[:, hs], queries[:, hs], grads[:, hs]
            s = nt(k, q) * scaling - slopes_ref[h] * far_ref[...]
            p = jnp.exp(s - stats[pl.ds(h, 1), :])
            ds = (p * (nt(values[:, hs], g) - stats[pl.ds(heads + h, 1), :])).astype(BF16)
            if to_query:
                part = tn(k, ds)
                dqt_ref[h] = part if first else dqt_ref[h] + part
            if to_key:
                kpart = nn(ds, q)
                vpart = nn(p.astype(BF16), g)
                dka_ref[h] = kpart if first else dka_ref[h] + kpart
                dva_ref[h] = vpart if first else dva_ref[h] + vpart

    parity = gather.parity
    near = 1 - 2 * parity
    home = REACH

    def to_query(slot, offset):
        visit(
            kv_ref.at[slot, 0], kv_ref.at[slot, 1], q_ref, og_ref, stats_ref,
            home + offset, home, True, False, False,
        )

    def to_key(slot, offset):
        visit(
            k_ref, v_ref, qbuf_ref.at[slot], obuf_ref.at[slot], sbuf_ref.at[slot],
            home, home + offset, False, True, False,
        )

    visit(k_ref, v_ref, q_ref, og_ref, stats_ref, home, home, True, True, True)
    to_query(0, -2)
    to_query(1, 2)
    for i in range(1 + CHUNKS):
        gather.relay(i)
    to_query(2, near)
    for i in range(1 + CHUNKS, len(gather.pieces)):
        gather.relay(i)
    to_query(3, -near)
    for h in range(heads):
        dq_ref[:, h * size : (h + 1) * size] = (dqt_ref[h].T * scaling).astype(BF16)
    to_key(1 - parity, 2 * near)
    gather.arrived(2)
    to_key(2, near)
    gather.arrived(parity)
    to_key(parity, -2 * near)
    gather.arrived(3)
    to_key(3, -near)
    for h in range(heads):
        hs = slice(h * size, (h + 1) * size)
        dk_ref[:, hs] = (dka_ref[h] * scaling).astype(BF16)
        dv_ref[:, hs] = dva_ref[h].astype(BF16)
    gather.sent()


def on_device(
    queries, keys, values, upstream, out_weight, slopes, patch_index, pair_lists, pair_counts
):
    n = lax.axis_size("ctx")
    nf = lax.axis_size("fsdp")
    me = lax.axis_index("ctx")
    tokens, width = queries.shape[1:]
    model = upstream.shape[2]
    heads = slopes.shape[0]
    size = width // heads
    blocks = tokens // BLOCK
    window = 2 * REACH + 1
    slots = window * blocks
    mask_rows = -(-slots // 8) * 8

    positions = patch_index[0]
    around = lax.dynamic_slice_in_dim(
        jnp.concatenate([positions, positions]), lax.rem(me + n - REACH, n) * tokens, window * tokens
    )
    rows_cols = jnp.stack([around // GRID, around % GRID]).astype(F32)
    wrow = jnp.pad(rows_cols, ((0, 6), (0, 0)))
    wcol = wrow.T
    pairs = pair_lists[0]
    listed = jnp.arange(pairs.shape[1]) < pair_counts[0, 0]
    hit = (
        listed[None, None, :]
        & (pairs[0][None, None, :] == jnp.arange(blocks)[None, :, None])
        & (pairs[1][None, None, :] == jnp.arange(mask_rows)[:, None, None])
    )
    block_mask = jnp.any(hit, axis=2).astype(F32)
    mask = jnp.broadcast_to(block_mask[:, :, None], (mask_rows, blocks, BLOCK)).reshape(
        mask_rows, tokens
    )

    vmem = pl.BlockSpec(memory_space=pltpu.VMEM)
    smem = pl.BlockSpec(memory_space=pltpu.SMEM)
    block = jax.ShapeDtypeStruct((tokens, width), BF16)
    q, k, v = queries[0], keys[0], values[0]
    pair_flops = 2 * tokens * tokens * window * width
    stat_rows = 2 * heads + mask_rows
    pieces = 2 * CHUNKS
    kv, og, att, stats = pl.pallas_call(
        functools.partial(forward_kernel, heads),
        out_shape=(
            jax.ShapeDtypeStruct((4, 2, tokens, width), BF16),
            block,
            block,
            jax.ShapeDtypeStruct((stat_rows, tokens), F32),
        ),
        in_specs=[smem] + [vmem] * 8,
        out_specs=(vmem,) * 4,
        scratch_shapes=[
            pltpu.VMEM((nf - 1,) + out_weight.shape, BF16),
            pltpu.VMEM((tokens, tokens), F32),
            pltpu.VMEM((heads, 1, tokens), F32),
            pltpu.VMEM((heads, 1, tokens), F32),
            pltpu.VMEM((heads, size, tokens), F32),
            pltpu.SemaphoreType.DMA((pieces, 4)),
            pltpu.SemaphoreType.DMA((pieces, 4)),
            pltpu.SemaphoreType.DMA((nf - 1,)),
            pltpu.SemaphoreType.DMA((nf - 1,)),
        ],
        compiler_params=pltpu.CompilerParams(
            collective_id=0, has_side_effects=True, vmem_limit_bytes=48 * 2**20
        ),
        cost_estimate=pl.CostEstimate(
            flops=2 * pair_flops, bytes_accessed=100 * 2**20, transcendentals=0
        ),
        name="forward",
    )(slopes, q, k, v, upstream[0], out_weight, wrow, wcol, mask)

    partial = (
        lax.dot_general(att, upstream[0], (((0,), (0,)), ((), ())), preferred_element_type=F32)
        .astype(BF16)
        .reshape(nf, width // nf, n, model // n)
        .transpose(0, 2, 1, 3)
        .reshape(nf * n, width // nf, model // n)
    )
    weight_grad = lax.psum_scatter(
        partial, ("fsdp", "ctx"), scatter_dimension=0, tiled=False
    ).astype(F32) / math.sqrt(tokens * n * nf)

    pieces = 2 * CHUNKS + 1
    dq, dk, dv = pl.pallas_call(
        functools.partial(backward_kernel, heads),
        out_shape=(block,) * 3,
        in_specs=[smem] + [vmem] * 8,
        out_specs=(vmem,) * 3,
        scratch_shapes=[
            pltpu.VMEM((4, tokens, width), BF16),
            pltpu.VMEM((4, tokens, width), BF16),
            pltpu.VMEM((4, stat_rows, tokens), F32),
            pltpu.VMEM((tokens, tokens), F32),
            pltpu.VMEM((heads, size, tokens), F32),
            pltpu.VMEM((heads, tokens, size), F32),
            pltpu.VMEM((heads, tokens, size), F32),
            pltpu.SemaphoreType.DMA((pieces, 4)),
            pltpu.SemaphoreType.DMA((pieces, 4)),
        ],
        compiler_params=pltpu.CompilerParams(
            collective_id=1, has_side_effects=True, vmem_limit_bytes=48 * 2**20
        ),
        cost_estimate=pl.CostEstimate(
            flops=8 * pair_flops, bytes_accessed=300 * 2**20, transcendentals=0
        ),
        name="backward",
    )(slopes, q, k, v, og, stats, kv, wrow, wcol)
    return (dq[None], dk[None], dv[None], weight_grad)


def solution(mesh):
    in_specs = (
        P("fsdp", "ctx", None),
        P("fsdp", "ctx", None),
        P("fsdp", "ctx", None),
        P("fsdp", "ctx", None),
        P("fsdp", None),
        P(),
        P("fsdp", None),
        P("fsdp", None, "ctx"),
        P("fsdp", "ctx"),
    )
    out_specs = (
        P("fsdp", "ctx", None),
        P("fsdp", "ctx", None),
        P("fsdp", "ctx", None),
        P("fsdp", "ctx"),
    )
    return jax.shard_map(
        on_device, mesh=mesh, in_specs=in_specs, out_specs=out_specs, check_vma=False
    )
```

time: 379 us -> 314 us (0.83); the launches traced: 373 us -> 314 us
  Pallas kernels: 0 us -> 247 us
  waiting for transfers between devices: 159 us -> 28.3 us
  matrix products: 97.4 us -> 2.42 us
  local copies, waits for them, and re-layouts: 56.7 us -> 18.2 us
  other arithmetic: 27.5 us -> 2.79 us
  starting transfers between devices: 17.1 us -> 0.04 us
    pallas_call x0 -> x2, Pallas kernels: none -> 247 us  [the longest x1 146 us: on_device(): pl.pallas_call(functools.partial(backward_kernel, heads), out_shape=(bloc...]
    ppermute x8 -> x0, waiting for transfers between devices: 123 us -> none  [passed_along(): return lax.ppermute(block, axis, route)]
    dot_general x33 -> x1, matrix products: 97.4 us -> 2.42 us  [on_device(): lax.dot_general(att, upstream[0], (((0,), (0,)), ((), ())), preferred_ele...]
    another operation x11 -> x2, local copies, waits for them, and re-layouts: 22.9 us -> 0.01 us  [on_device(): rows_cols = jnp.stack([around // GRID, around % GRID]).astype(F32)]
    ppermute x8 -> x0, starting transfers between devices: 17 us -> none  [passed_along(): return lax.ppermute(block, axis, route)]
    another operation x6 -> x0, other arithmetic: 16 us -> none  [the longest x4 8.82 us: on_device(): jnp.stack([key_part, value_part]).reshape(2, token_count, inner_width)]
    slice x6 -> x0, local copies, waits for them, and re-layouts: 8.56 us -> none  [the longest x4 7.22 us: on_device(): value_heads = arrived[1].reshape(token_count, head_count, head_size)]
    reduce_scatter x2 -> x1, waiting for transfers between devices: 35.7 us -> 28.3 us  [on_device(): lax.psum_scatter(partial, ('fsdp', 'ctx'), scatter_dimension=0, tiled=False)]
  transfers between devices with their start and end apart: 11 -> 1, of which waited for: 7 -> 1; matrix products, arithmetic and copies ran while one was open for 37% -> 0% of each run, Pallas kernels for 0% -> 47%
where the time goes in v1:
time: 314 us
  Pallas kernels  247 us (79%)
  waiting for transfers between devices  28.3 us (9%)
  local copies, waits for them, and re-layouts  18.2 us (6%)
  between operations  14.9 us (5%)
    pallas_call x1, Pallas kernels, on_device(): pl.pallas_call(functools.partial(backward_kernel, heads), out_shape=(bloc...  146 us
    pallas_call x1, Pallas kernels, on_device(): pl.pallas_call(functools.partial(forward_kernel, heads), out_shape=(jax.S...  101 us
    reduce_scatter x1, waiting for transfers between devices, on_device(): lax.psum_scatter(partial, ('fsdp', 'ctx'), scatter_dimension=0, tiled=False)  28.3 us
    unnamed x28, local copies, waits for them, and re-layouts  11.3 us
  transfers between devices with their start and end apart: 1, of which 1 were waited for; matrix products, arithmetic and copies ran while one was open for 0% of the time, Pallas kernels for 47%

profile of v1, /device:TPU:0, one launch (start us, length us, event | category | flops | bytes accessed | tf_op | source)
XLA Modules:
  0.0 313.8 jit_solution(2578802579300599665)
XLA Ops:
  7.2 0.0 copy-start.7
  7.2 0.0 copy-start.1
  7.2 0.0 copy-start.2
  7.2 0.0 reduce-scatter.2.cloned.1.call-start
  7.3 1.0 add_select_fusion.1
  8.3 1.3 copy.30
  9.6 1.5 copy.38
  11.1 1.3 pad_bitcast_fusion.wcol_ref
  13.1 0.8 slice_bitcast_fusion.1
  13.8 0.1 and_reduce_fusion
  14.0 0.1 copy.31
  14.1 0.1 broadcast_in_dim.8
  14.2 0.0 copy-start.3
  14.2 1.1 copy-done.3
  15.4 1.1 copy-done.5
  16.5 101.2 %forward.1 = (bf16[4,2,384,1024]{3,2,1,0:T(8,128)(2,1)}, bf16[384,1024]{1,0:T(8,128)(2,1)S(1)}, bf16[384,1024]{1,0:T(8,128)(2,1)S(1)}, f32[32,384]{1,0:T(8,128)S(1)}) custom-call(f32[8]{0:T(128)S(1)} %copy-done.7, bf16[384,1024]{1,0:T(8,128)(2,1)S(1)} %bitcast.37, bf16[384,1024]{1,0:T(8,128)(2,1)S(1)} %bitcast.39, bf16[384,1024]{1,0:T(8,128)(2,1)S(1)} %bitcast.41, ...), custom_call_target="tpu_custom_call" | custom-call | flops 3019898880 | bytes 104857600 | tf_op jit(solution)/shard_map/forward/pallas_call | solution.py:388
  117.8 0.0 copy-start.8
  117.8 2.4 convolution_convert_fusion
  120.2 1.5 copy.36
  121.7 0.3 bitcast_bitcast_fusion
  122.0 3.0 copy.34
  125.0 0.0 reduce-scatter.2.cloned.1.call-update
  125.0 0.0 copy-start.4
  125.1 1.1 copy-done.4
  126.2 1.1 copy-done.6
  127.3 1.1 copy-done.9
  128.4 146.0 %backward.1 = (bf16[384,1024]{1,0:T(8,128)(2,1)S(1)}, bf16[384,1024]{1,0:T(8,128)(2,1)S(1)}, bf16[384,1024]{1,0:T(8,128)(2,1)S(1)}) custom-call(f32[8]{0:T(128)S(1)} %copy-done.7, bf16[384,1024]{1,0:T(8,128)(2,1)S(1)} %bitcast.38, bf16[384,1024]{1,0:T(8,128)(2,1)S(1)} %bitcast.40, bf16[384,1024]{1,0:T(8,128)(2,1)S(1)} %bitcast.42, ...), custom_call_target="tpu_custom_call" | custom-call | flops 12079595520 | bytes 314572800 | tf_op jit(solution)/shard_map/backward/pallas_call | solution.py:430
  274.4 28.3 %reduce-scatter.2.cloned.1.call-done = bf16[1,256,256]{2,1,0:T(8,128)(2,1)} async-done(((bf16[32,256,256]{2,1,0:T(8,128)(2,1)}), bf16[1,256,256]{2,1,0:T(8,128)(2,1)}) %reduce-scatter.2.cloned.1.call-update) | async-done | bytes 131088 | tf_op jit(solution)/shard_map/reduce_scatter | solution.py:425
  302.7 1.6 multiply_bitcast_fusion
  304.3 0.9 copy.44
  305.2 0.9 copy.45
  306.1 0.9 copy.46
  (20 shorter events, 0.1 us)
Async XLA Ops:
  7.2 7.0 %copy-start.7 = (f32[8]{0:T(128)S(1)}, f32[8]{0:T(128)}, u32[]{:S(2)}) copy-start(f32[8]{0:T(128)} %slopes_ref.3) | copy-start | bytes 100
  7.2 7.0 %copy-start.1 = (bf16[256,2048]{1,0:T(8,128)(2,1)S(1)}, bf16[256,2048]{1,0:T(8,128)(2,1)}, u32[]{:S(2)}) copy-start(bf16[256,2048]{1,0:T(8,128)(2,1)} %w_ref.1) | copy-start | bytes 3145732
  7.2 7.0 %copy-start.2 = (bf16[1,384,1024]{2,1,0:T(8,128)(2,1)S(1)}, bf16[1,384,1024]{2,1,0:T(8,128)(2,1)}, u32[]{:S(2)}) copy-start(bf16[1,384,1024]{2,1,0:T(8,128)(2,1)} %param.9) | copy-start | bytes 2359300
  7.2 295.5 %reduce-scatter.2.cloned.1.call-start = ((), (), s32[]{:S(2)}) async-start(), calls=%async_computation.1 | async-start | bytes 4325376 | tf_op jit(solution)/shard_map/reduce_scatter | solution.py:425
  12.4 105.4 %copy-start = (f32[1920,8]{1,0:T(8,128)}, f32[1920,8]{1,0:T(8,128)S(1)}, u32[]{:S(2)}) copy-start(f32[1920,8]{1,0:T(8,128)S(1)} %pad_bitcast_fusion.wcol_ref) | copy-start | bytes 184324
  14.2 1.1 copy-start.3
  15.4 1.1 copy-start.5
  16.5 101.3 %copy-start.10 = (bf16[1,384,2048]{2,1,0:T(8,128)(2,1)S(1)}, bf16[1,384,2048]{2,1,0:T(8,128)(2,1)}, u32[]{:S(2)}) copy-start(bf16[1,384,2048]{2,1,0:T(8,128)(2,1)} %param.12) | copy-start | bytes 4718596
  117.8 2.5 copy-start.8
  125.0 1.1 copy-start.4
  126.2 1.1 copy-start.6
  127.3 1.1 copy-start.9
Sparse Core Ops, SparseCore 0:
  125.2 177.5 reduce-scatter.1

commit v2 on v1

--- a/solution.py
+++ b/solution.py
@@ -48,9 +48,6 @@
         self.pieces = pieces
         self.send_sem = send_sem
         self.recv_sem = recv_sem
-
-    def targets(self):
-        return [{"ctx": self.up}, {"ctx": self.down}, {"ctx": self.partner}]
 
     def copy(self, i, slot):
         own, land = self.pieces[i]
@@ -65,8 +62,8 @@
             device_id_type=MESH,
         )
 
-    def start(self):
-        for i in range(len(self.pieces)):
+    def start(self, pieces):
+        for i in pieces:
             for slot in (0, 1, 2):
                 self.copy(i, slot).start()
 
@@ -83,8 +80,8 @@
         ).wait_recv()
         self.copy(i, 3).start()
 
-    def arrived(self, slot):
-        for i in range(len(self.pieces)):
+    def arrived(self, slot, pieces):
+        for i in pieces:
             own, land = self.pieces[i]
             pltpu.make_async_remote_copy(
                 src_ref=own,
@@ -101,6 +98,12 @@
                 self.copy(i, slot).wait_send()
 
 
+def remote(src, dst, send_sem, recv_sem, target):
+    return pltpu.make_async_remote_copy(
+        src_ref=src, dst_ref=dst, send_sem=send_sem, recv_sem=recv_sem, device_id=target, device_id_type=MESH
+    )
+
+
 def row_pieces(own_ref, land_ref, index, chunks):
     rows = own_ref.shape[0] // chunks
 
@@ -130,8 +133,9 @@
     return pl.ds(pl.multiple_of(h * size, size), size)
 
 
-def forward_kernel(
+def fused_kernel(
     heads,
+    weight_scale,
     slopes_ref,
     q_ref,
     k_ref,
@@ -141,7 +145,14 @@
     wrow_ref,
     wcol_ref,
     mask_ref,
+    dq_ref,
+    dk_ref,
+    dv_ref,
+    wg_ref,
     kv_ref,
+    qbuf_ref,
+    obuf_ref,
+    sbuf_ref,
     og_ref,
     att_ref,
     stats_ref,
@@ -150,34 +161,58 @@
     top_ref,
     total_ref,
     acc_ref,
+    dka_ref,
+    dva_ref,
+    part_ref,
+    pland_ref,
+    wsum_ref,
+    ysum_ref,
+    zland_ref,
     send_sem,
     recv_sem,
     wsend_sem,
     wrecv_sem,
+    gsend_sem,
+    grecv_sem,
+    ysem,
+    zsend_sem,
+    zrecv_sem,
 ):
     tokens, width = q_ref.shape
     size = width // heads
     blocks = tokens // BLOCK
     scaling = 1.0 / math.sqrt(size)
+    n = lax.axis_size("ctx")
     nf = lax.axis_size("fsdp")
+    me = lax.axis_index("ctx")
     fs = lax.axis_index("fsdp")
     wrows = w_ref.shape[0]
+    model = up_ref.shape[1]
+    half = n // 2
+    wide = wsum_ref.shape[3]
+    kv_pieces = range(0, 2 * CHUNKS)
+    q_pieces = range(2 * CHUNKS, 3 * CHUNKS)
+    o_pieces = range(3 * CHUNKS, 4 * CHUNKS)
+    s_pieces = range(4 * CHUNKS, 4 * CHUNKS + 1)
+    late_pieces = range(2 * CHUNKS, 4 * CHUNKS + 1)
     gather = Gather(
-        row_pieces(k_ref, kv_ref, 0, CHUNKS) + row_pieces(v_ref, kv_ref, 1, CHUNKS),
+        row_pieces(k_ref, kv_ref, 0, CHUNKS)
+        + row_pieces(v_ref, kv_ref, 1, CHUNKS)
+        + row_pieces(q_ref, qbuf_ref, None, CHUNKS)
+        + row_pieces(og_ref, obuf_ref, None, CHUNKS)
+        + row_pieces(stats_ref, sbuf_ref, None, 1),
         send_sem,
         recv_sem,
     )
-    greet(gather.targets() + [{"fsdp": lax.rem(fs + d, nf)} for d in range(1, nf)])
-    gather.start()
+    parity = gather.parity
+    near = 1 - 2 * parity
+    home = REACH
+    others = [{"fsdp": lax.rem(fs + d, nf)} for d in range(1, nf)]
+    across = [{"ctx": lax.rem(me + 2 * d, n)} for d in range(1, half)]
+    greet([{"ctx": gather.partner}] + across + others)
+    gather.start(kv_pieces)
     wcopies = [
-        pltpu.make_async_remote_copy(
-            src_ref=w_ref,
-            dst_ref=wbuf_ref.at[d - 1],
-            send_sem=wsend_sem.at[d - 1],
-            recv_sem=wrecv_sem.at[d - 1],
-            device_id={"fsdp": lax.rem(fs + d, nf)},
-            device_id_type=MESH,
-        )
+        remote(w_ref, wbuf_ref.at[d - 1], wsend_sem.at[d - 1], wrecv_sem.at[d - 1], others[d - 1])
         for d in range(1, nf)
     ]
     for copy in wcopies:
@@ -187,13 +222,13 @@
     total_ref[...] = jnp.zeros(total_ref.shape, F32)
     acc_ref[...] = jnp.zeros(acc_ref.shape, F32)
 
-    def visit(keys, values, offset):
+    def look(keys, values, offset):
         at = offset + REACH
 
         def mask_row(b):
             return mask_ref[pl.ds(at * blocks + b, 1), :]
 
-        build_distance(far_ref, wrow_ref, wcol_ref, at, REACH, mask_row, tokens)
+        build_distance(far_ref, wrow_ref, wcol_ref, at, home, mask_row, tokens)
 
         @pl.loop(0, heads)
         def _(h):
@@ -207,79 +242,50 @@
             total_ref[h] = total_ref[h] * factor + jnp.sum(p, axis=0, keepdims=True)
             acc_ref[h] = acc_ref[h] * factor + tn(values[:, hs], p.astype(BF16))
 
-    def visit_slot(slot, offset):
-        visit(kv_ref.at[slot, 0], kv_ref.at[slot, 1], offset)
+    def look_slot(slot, offset):
+        look(kv_ref.at[slot, 0], kv_ref.at[slot, 1], offset)
 
     def project(block, owner):
         cols = pl.ds(pl.multiple_of(owner * wrows, BLOCK), wrows)
         og_ref[:, cols] = nt(up_ref[...], block[...]).astype(BF16)
 
-    parity = gather.parity
-    near = 1 - 2 * parity
-    visit(k_ref, v_ref, 0)
+    look(k_ref, v_ref, 0)
     project(w_ref, fs)
-    for i in range(len(gather.pieces)):
+    for i in kv_pieces:
         gather.relay(i)
-    visit_slot(1 - parity, 2 * near)
-    gather.arrived(2)
-    visit_slot(2, near)
+    gather.start(q_pieces)
+    look_slot(1 - parity, 2 * near)
     for d in range(1, nf):
         wcopies[d - 1].wait()
         project(wbuf_ref.at[d - 1], lax.rem(fs + nf - d, nf))
-    gather.arrived(parity)
-    visit_slot(parity, -2 * near)
-    gather.arrived(3)
-    visit_slot(3, -near)
+    gather.start(o_pieces)
+    gather.arrived(2, kv_pieces)
+    look_slot(2, near)
+    gather.arrived(parity, kv_pieces)
+    look_slot(parity, -2 * near)
+    gather.arrived(3, kv_pieces)
+    look_slot(3, -near)
     for h in range(heads):
         hs = slice(h * size, (h + 1) * size)
         total = total_ref[h]
-        att_t = acc_ref[h] / total
-        att = att_t.T.astype(BF16)
+        att = (acc_ref[h] / total).T.astype(BF16)
         att_ref[:, hs] = att
         stats_ref[h : h + 1, :] = top_ref[h] + jnp.log(total)
         prod = og_ref[:, hs].astype(F32) * att.astype(F32)
         stats_ref[heads + h : heads + h + 1, :] = jnp.sum(prod.T, axis=0, keepdims=True)
     stats_ref[2 * heads :, :] = mask_ref[...]
-    gather.sent()
-
-
-def backward_kernel(
-    heads,
-    slopes_ref,
-    q_ref,
-    k_ref,
-    v_ref,
-    og_ref,
-    stats_ref,
-    kv_ref,
-    wrow_ref,
-    wcol_ref,
-    dq_ref,
-    dk_ref,
-    dv_ref,
-    qbuf_ref,
-    obuf_ref,
-    sbuf_ref,
-    far_ref,
-    dqt_ref,
-    dka_ref,
-    dva_ref,
-    send_sem,
-    recv_sem,
-):
-    tokens, width = q_ref.shape
-    size = width // heads
-    blocks = tokens // BLOCK
-    scaling = 1.0 / math.sqrt(size)
-    gather = Gather(
-        row_pieces(stats_ref, sbuf_ref, None, 1)
-        + row_pieces(q_ref, qbuf_ref, None, CHUNKS)
-        + row_pieces(og_ref, obuf_ref, None, CHUNKS),
-        send_sem,
-        recv_sem,
-    )
-    greet(gather.targets())
-    gather.start()
+    gather.start(s_pieces)
+
+    gcopies = []
+    for d in range(1, nf):
+        owner = lax.rem(fs + d, nf)
+        cols = pl.ds(pl.multiple_of(owner * wrows, BLOCK), wrows)
+        part_ref[d - 1] = tn(att_ref[:, cols], up_ref[...]).astype(BF16)
+        copy = remote(
+            part_ref.at[d - 1], pland_ref.at[d - 1], gsend_sem.at[d - 1], grecv_sem.at[d - 1], others[d - 1]
+        )
+        copy.start()
+        gcopies.append(copy)
 
     def visit(keys, values, queries, grads, stats, key_at, query_at, to_query, to_key, first):
         def mask_row(b):
@@ -296,17 +302,13 @@
             ds = (p * (nt(values[:, hs], g) - stats[pl.ds(heads + h, 1), :])).astype(BF16)
             if to_query:
                 part = tn(k, ds)
-                dqt_ref[h] = part if first else dqt_ref[h] + part
+                acc_ref[h] = part if first else acc_ref[h] + part
             if to_key:
                 kpart = nn(ds, q)
                 vpart = nn(p.astype(BF16), g)
                 dka_ref[h] = kpart if first else dka_ref[h] + kpart
                 dva_ref[h] = vpart if first else dva_ref[h] + vpart
 
-    parity = gather.parity
-    near = 1 - 2 * parity
-    home = REACH
-
     def to_query(slot, offset):
         visit(
             kv_ref.at[slot, 0], kv_ref.at[slot, 1], q_ref, og_ref, stats_ref,
@@ -319,28 +321,66 @@
             home, home + offset, False, True, False,
         )
 
+    for i in q_pieces:
+        gather.relay(i)
     visit(k_ref, v_ref, q_ref, og_ref, stats_ref, home, home, True, True, True)
     to_query(0, -2)
+    for i in o_pieces:
+        gather.relay(i)
     to_query(1, 2)
-    for i in range(1 + CHUNKS):
+    for i in s_pieces:
         gather.relay(i)
     to_query(2, near)
-    for i in range(1 + CHUNKS, len(gather.pieces)):
-        gather.relay(i)
     to_query(3, -near)
     for h in range(heads):
-        dq_ref[:, h * size : (h + 1) * size] = (dqt_ref[h].T * scaling).astype(BF16)
+        dq_ref[:, h * size : (h + 1) * size] = (acc_ref[h].T * scaling).astype(BF16)
+
+    mine = tn(att_ref[:, pl.ds(pl.multiple_of(fs * wrows, BLOCK), wrows)], up_ref[...])
+    for copy in gcopies:
+        copy.wait()
+    for d in range(1, nf):
+        mine = mine + pland_ref[d - 1].astype(F32)
+    for c in range(n):
+        at = c * (model // n) // wide * wide
+        wsum_ref[c % 2, c // 2] = mine[:, at : at + wide].astype(BF16)
+    ycopy = remote(
+        wsum_ref.at[1 - parity], ysum_ref, ysem.at[0], ysem.at[1], {"ctx": gather.partner}
+    )
+    ycopy.start()
+
     to_key(1 - parity, 2 * near)
-    gather.arrived(2)
+    gather.arrived(2, late_pieces)
     to_key(2, near)
-    gather.arrived(parity)
+
+    ycopy.wait()
+    row = lax.div(me, 2)
+    zcopies = []
+    for d in range(half):
+        k = lax.rem(row + d, half)
+        pair_sum = wsum_ref[parity, k].astype(F32) + ysum_ref[k].astype(F32)
+        if d == 0:
+            wg_ref[...] = pair_sum
+            continue
+        zland_ref[0, d - 1] = pair_sum.astype(BF16)
+        copy = remote(
+            zland_ref.at[0, d - 1], zland_ref.at[1, d - 1], zsend_sem.at[d - 1], zrecv_sem.at[d - 1], across[d - 1]
+        )
+        copy.start()
+        zcopies.append(copy)
+
+    gather.arrived(parity, late_pieces)
     to_key(parity, -2 * near)
-    gather.arrived(3)
+    gather.arrived(3, late_pieces)
     to_key(3, -near)
     for h in range(heads):
         hs = slice(h * size, (h + 1) * size)
         dk_ref[:, hs] = (dka_ref[h] * scaling).astype(BF16)
         dv_ref[:, hs] = dva_ref[h].astype(BF16)
+    total = wg_ref[...]
+    for d in range(1, half):
+        zcopies[d - 1].wait()
+        total = total + zland_ref[1, d - 1].astype(F32)
+    wg_ref[...] = total * weight_scale
     gather.sent()
 
 
@@ -381,76 +421,58 @@
     vmem = pl.BlockSpec(memory_space=pltpu.VMEM)
     smem = pl.BlockSpec(memory_space=pltpu.SMEM)
     block = jax.ShapeDtypeStruct((tokens, width), BF16)
-    q, k, v = queries[0], keys[0], values[0]
     pair_flops = 2 * tokens * tokens * window * width
     stat_rows = 2 * heads + mask_rows
-    pieces = 2 * CHUNKS
-    kv, og, att, stats = pl.pallas_call(
-        functools.partial(forward_kernel, heads),
-        out_shape=(
-            jax.ShapeDtypeStruct((4, 2, tokens, width), BF16),
-            block,
-            block,
-            jax.ShapeDtypeStruct((stat_rows, tokens), F32),
-        ),
+    pieces = 4 * CHUNKS + 1
+    wrows = out_weight.shape[0]
+    cut = model // n
+    wide = max(cut, BLOCK)
+    half = n // 2
+    dq, dk, dv, weight_grad = pl.pallas_call(
+        functools.partial(fused_kernel, heads, 1.0 / math.sqrt(tokens * n * nf)),
+        out_shape=(block, block, block, jax.ShapeDtypeStruct((wrows, wide), F32)),
         in_specs=[smem] + [vmem] * 8,
         out_specs=(vmem,) * 4,
         scratch_shapes=[
+            pltpu.VMEM((4, 2, tokens, width), BF16),
+            pltpu.VMEM((4, tokens, width), BF16),
+            pltpu.VMEM((4, tokens, width), BF16),
+            pltpu.VMEM((4, stat_rows, tokens), F32),
+            pltpu.VMEM((tokens, width), BF16),
+            pltpu.VMEM((tokens, width), BF16),
+            pltpu.VMEM((stat_rows, tokens), F32),
             pltpu.VMEM((nf - 1,) + out_weight.shape, BF16),
             pltpu.VMEM((tokens, tokens), F32),
             pltpu.VMEM((heads, 1, tokens), F32),
             pltpu.VMEM((heads, 1, tokens), F32),
             pltpu.VMEM((heads, size, tokens), F32),
+            pltpu.VMEM((heads, tokens, size), F32),
+            pltpu.VMEM((heads, tokens, size), F32),
+            pltpu.VMEM((nf - 1, wrows, model), BF16),
+            pltpu.VMEM((nf - 1, wrows, model), BF16),
+            pltpu.VMEM((2, half, wrows, wide), BF16),
+            pltpu.VMEM((half, wrows, wide), BF16),
+            pltpu.VMEM((2, half - 1, wrows, wide), BF16),
             pltpu.SemaphoreType.DMA((pieces, 4)),
             pltpu.SemaphoreType.DMA((pieces, 4)),
             pltpu.SemaphoreType.DMA((nf - 1,)),
             pltpu.SemaphoreType.DMA((nf - 1,)),
+            pltpu.SemaphoreType.DMA((nf - 1,)),
+            pltpu.SemaphoreType.DMA((nf - 1,)),
+            pltpu.SemaphoreType.DMA((2,)),
+            pltpu.SemaphoreType.DMA((half - 1,)),
+            pltpu.SemaphoreType.DMA((half - 1,)),
         ],
         compiler_params=pltpu.CompilerParams(
-            collective_id=0, has_side_effects=True, vmem_limit_bytes=48 * 2**20
+            collective_id=0, has_side_effects=True, vmem_limit_bytes=58 * 2**20
         ),
         cost_estimate=pl.CostEstimate(
-            flops=2 * pair_flops, bytes_accessed=100 * 2**20, transcendentals=0
+            flops=10 * pair_flops, bytes_accessed=400 * 2**20, transcendentals=0
         ),
-        name="forward",
-    )(slopes, q, k, v, upstream[0], out_weight, wrow, wcol, mask)
-
-    partial = (
-        lax.dot_general(att, upstream[0], (((0,), (0,)), ((), ())), preferred_element_type=F32)
-        .astype(BF16)
-        .reshape(nf, width // nf, n, model // n)
-        .transpose(0, 2, 1, 3)
-        .reshape(nf * n, width // nf, model // n)
-    )
-    weight_grad = lax.psum_scatter(
-        partial, ("fsdp", "ctx"), scatter_dimension=0, tiled=False
-    ).astype(F32) / math.sqrt(tokens * n * nf)
-
-    pieces = 2 * CHUNKS + 1
-    dq, dk, dv = pl.pallas_call(
-        functools.partial(backward_kernel, heads),
-        out_shape=(block,) * 3,
-        in_specs=[smem] + [vmem] * 8,
-        out_specs=(vmem,) * 3,
-        scratch_shapes=[
-            pltpu.VMEM((4, tokens, width), BF16),
-            pltpu.VMEM((4, tokens, width), BF16),
-            pltpu.VMEM((4, stat_rows, tokens), F32),
-            pltpu.VMEM((tokens, tokens), F32),
-            pltpu.VMEM((heads, size, tokens), F32),
-            pltpu.VMEM((heads, tokens, size), F32),
-            pltpu.VMEM((heads, tokens, size), F32),
-            pltpu.SemaphoreType.DMA((pieces, 4)),
-            pltpu.SemaphoreType.DMA((pieces, 4)),
-        ],
-        compiler_params=pltpu.CompilerParams(
-            collective_id=1, has_side_effects=True, vmem_limit_bytes=48 * 2**20
-        ),
-        cost_estimate=pl.CostEstimate(
-            flops=8 * pair_flops, bytes_accessed=300 * 2**20, transcendentals=0
-        ),
-        name="backward",
-    )(slopes, q, k, v, og, stats, kv, wrow, wcol)
+        name="fused",
+    )(slopes, queries[0], keys[0], values[0], upstream[0], out_weight, wrow, wcol, mask)
+    if wide > cut:
+        weight_grad = lax.dynamic_slice_in_dim(weight_grad, me * cut % wide, cut, 1)
     return (dq[None], dk[None], dv[None], weight_grad)
 
 

time: 314 us -> 195 us (0.62)
  Pallas kernels: 247 us -> 183 us
  waiting for transfers between devices: 28.3 us -> 0 us
  between operations: 14.9 us -> 1.37 us
  local copies, waits for them, and re-layouts: 18.2 us -> 8.57 us
    pallas_call x2 -> x1, Pallas kernels: 247 us -> 183 us  [on_device(): pl.pallas_call(functools.partial(fused_kernel, heads, 1.0 / math.sqrt(tok...]
    reduce_scatter x1 -> x0, waiting for transfers between devices: 28.3 us -> none  [on_device(): lax.psum_scatter(partial, ('fsdp', 'ctx'), scatter_dimension=0, tiled=False)]
    unnamed x28 -> x12, local copies, waits for them, and re-layouts: 11.3 us -> 5.59 us
    transpose x2 -> x0, local copies, waits for them, and re-layouts: 3.3 us -> none  [on_device(): partial = lax.dot_general(att, upstream[0], (((0,), (0,)), ((), ())), pre...]
  transfers between devices with their start and end apart: 1 -> 0, of which waited for: 1 -> 0; matrix products, arithmetic and copies ran while one was open for 0% -> 0% of each run, Pallas kernels for 47% -> 0%
where the time goes in v2:
time: 195 us; the launch traced here: 194 us
  Pallas kernels  183 us (94%)
  local copies, waits for them, and re-layouts  8.57 us (4%)
    pallas_call x1, Pallas kernels, on_device(): pl.pallas_call(functools.partial(fused_kernel, heads, 1.0 / math.sqrt(tok...  183 us
    unnamed x12, local copies, waits for them, and re-layouts  5.59 us

profile of v2, /device:TPU:0, one launch (start us, length us, event | category | flops | bytes accessed | tf_op | source)
XLA Modules:
  0.0 193.9 jit_solution(9288225216518331004)
XLA Ops:
  1.3 0.8 slice_bitcast_fusion.1
  2.1 0.1 and_reduce_fusion
  2.2 0.1 copy.23
  2.3 0.9 add_select_fusion.1
  3.3 0.1 broadcast_in_dim.8
  3.3 0.6 copy.28
  4.0 0.4 copy.22
  4.3 0.3 copy.27
  4.6 1.1 pad_bitcast_fusion.wcol_ref
  5.7 0.6 pad.4.clone.wrow_ref
  6.3 182.9 %fused.1 = (bf16[384,1024]{1,0:T(8,128)(2,1)}, bf16[384,1024]{1,0:T(8,128)(2,1)}, bf16[384,1024]{1,0:T(8,128)(2,1)}, f32[256,256]{1,0:T(8,128)}) custom-call(f32[8]{0:T(128)} %slopes_ref.1, bf16[384,1024]{1,0:T(8,128)(2,1)} %bitcast.27, bf16[384,1024]{1,0:T(8,128)(2,1)} %bitcast.28, bf16[384,1024]{1,0:T(8,128)(2,1)} %bitcast.29, bf16[384,2048]{1,0:T(8,128)(2,1)} %bitcast.26, ...), custom_call_target="tpu_custom_call" | custom-call | flops 15099494400 | bytes 419430400 | tf_op jit(solution)/shard_map/fused/pallas_call | solution.py:431
  189.2 0.0 copy-start.1
  189.3 0.0 copy-start
  189.3 2.2 %copy.34 = bf16[1,384,1024]{2,1,0:T(8,128)(2,1)} copy(bf16[1,384,1024]{2,1,0:T(8,128)(2,1)} %bitcast.22) | data formatting | bytes 1572864
  191.4 0.0 copy-done.1
  191.4 0.0 copy-start.2
  191.5 0.9 copy.35
  192.3 0.0 copy-done
  192.3 0.9 copy.36
  193.2 0.0 copy-done.2
  193.2 0.7 copy.37
  (7 shorter events, 0.1 us)
Async XLA Ops:
  189.2 2.2 %copy-start.1 = (bf16[384,1024]{1,0:T(8,128)(2,1)S(1)}, bf16[384,1024]{1,0:T(8,128)(2,1)}, u32[]{:S(2)}) copy-start(bf16[384,1024]{1,0:T(8,128)(2,1)} %get-tuple-element.9) | copy-start | bytes 2359300
  189.3 3.1 %copy-start = (bf16[384,1024]{1,0:T(8,128)(2,1)S(1)}, bf16[384,1024]{1,0:T(8,128)(2,1)}, u32[]{:S(2)}) copy-start(bf16[384,1024]{1,0:T(8,128)(2,1)} %get-tuple-element.10) | copy-start | bytes 2359300
  191.4 1.8 copy-start.2

commit v3 on v2

--- a/solution.py
+++ b/solution.py
@@ -207,16 +207,24 @@
     parity = gather.parity
     near = 1 - 2 * parity
     home = REACH
-    others = [{"fsdp": lax.rem(fs + d, nf)} for d in range(1, nf)]
+    twin = fs + 1 - 2 * lax.rem(fs, 2)
+    facing = lax.rem(fs + 2, nf)
+    corner = lax.rem(twin + 2, nf)
     across = [{"ctx": lax.rem(me + 2 * d, n)} for d in range(1, half)]
-    greet([{"ctx": gather.partner}] + across + others)
+    greet([{"ctx": gather.partner}] + across + [{"fsdp": twin}, {"fsdp": facing}])
     gather.start(kv_pieces)
     wcopies = [
-        remote(w_ref, wbuf_ref.at[d - 1], wsend_sem.at[d - 1], wrecv_sem.at[d - 1], others[d - 1])
-        for d in range(1, nf)
+        remote(
+            wbuf_ref.at[1] if d == 2 else w_ref,
+            wbuf_ref.at[d],
+            wsend_sem.at[d],
+            wrecv_sem.at[d],
+            {"fsdp": facing if d == 1 else twin},
+        )
+        for d in range(3)
     ]
-    for copy in wcopies:
-        copy.start()
+    wcopies[0].start()
+    wcopies[1].start()
 
     top_ref[...] = jnp.full(top_ref.shape, -1e30, F32)
     total_ref[...] = jnp.zeros(total_ref.shape, F32)
@@ -253,11 +261,16 @@
     project(w_ref, fs)
     for i in kv_pieces:
         gather.relay(i)
-    gather.start(q_pieces)
+        if i == CHUNKS - 1:
+            gather.start(q_pieces)
     look_slot(1 - parity, 2 * near)
-    for d in range(1, nf):
-        wcopies[d - 1].wait()
-        project(wbuf_ref.at[d - 1], lax.rem(fs + nf - d, nf))
+    wcopies[1].wait()
+    wcopies[2].start()
+    project(wbuf_ref.at[1], facing)
+    wcopies[0].wait()
+    project(wbuf_ref.at[0], twin)
+    wcopies[2].wait()
+    project(wbuf_ref.at[2], corner)
     gather.start(o_pieces)
     gather.arrived(2, kv_pieces)
     look_slot(2, near)
@@ -276,16 +289,24 @@
     stats_ref[2 * heads :, :] = mask_ref[...]
     gather.start(s_pieces)
 
-    gcopies = []
-    for d in range(1, nf):
-        owner = lax.rem(fs + d, nf)
+    def part_of(owner):
         cols = pl.ds(pl.multiple_of(owner * wrows, BLOCK), wrows)
-        part_ref[d - 1] = tn(att_ref[:, cols], up_ref[...]).astype(BF16)
-        copy = remote(
-            part_ref.at[d - 1], pland_ref.at[d - 1], gsend_sem.at[d - 1], grecv_sem.at[d - 1], others[d - 1]
+        return tn(att_ref[:, cols], up_ref[...])
+
+    gcopies = [
+        remote(
+            part_ref.at[d],
+            pland_ref.at[d],
+            gsend_sem.at[d],
+            grecv_sem.at[d],
+            {"fsdp": facing if d == 2 else twin},
         )
-        copy.start()
-        gcopies.append(copy)
+        for d in range(3)
+    ]
+    part_ref[1] = part_of(corner).astype(BF16)
+    gcopies[1].start()
+    part_ref[0] = part_of(twin).astype(BF16)
+    gcopies[0].start()
 
     def visit(keys, values, queries, grads, stats, key_at, query_at, to_query, to_key, first):
         def mask_row(b):
@@ -324,6 +345,9 @@
     for i in q_pieces:
         gather.relay(i)
     visit(k_ref, v_ref, q_ref, og_ref, stats_ref, home, home, True, True, True)
+    gcopies[1].wait()
+    part_ref[2] = (part_of(facing) + pland_ref[1].astype(F32)).astype(BF16)
+    gcopies[2].start()
     to_query(0, -2)
     for i in o_pieces:
         gather.relay(i)
@@ -335,11 +359,9 @@
     for h in range(heads):
         dq_ref[:, h * size : (h + 1) * size] = (acc_ref[h].T * scaling).astype(BF16)
 
-    mine = tn(att_ref[:, pl.ds(pl.multiple_of(fs * wrows, BLOCK), wrows)], up_ref[...])
-    for copy in gcopies:
-        copy.wait()
-    for d in range(1, nf):
-        mine = mine + pland_ref[d - 1].astype(F32)
+    gcopies[0].wait()
+    gcopies[2].wait()
+    mine = part_of(fs) + pland_ref[0].astype(F32) + pland_ref[2].astype(F32)
     for c in range(n):
         at = c * (model // n) // wide * wide
         wsum_ref[c % 2, c // 2] = mine[:, at : at + wide].astype(BF16)
@@ -441,24 +463,24 @@
             pltpu.VMEM((tokens, width), BF16),
             pltpu.VMEM((tokens, width), BF16),
             pltpu.VMEM((stat_rows, tokens), F32),
-            pltpu.VMEM((nf - 1,) + out_weight.shape, BF16),
+            pltpu.VMEM((3,) + out_weight.shape, BF16),
             pltpu.VMEM((tokens, tokens), F32),
             pltpu.VMEM((heads, 1, tokens), F32),
             pltpu.VMEM((heads, 1, tokens), F32),
             pltpu.VMEM((heads, size, tokens), F32),
             pltpu.VMEM((heads, tokens, size), F32),
             pltpu.VMEM((heads, tokens, size), F32),
-            pltpu.VMEM((nf - 1, wrows, model), BF16),
-            pltpu.VMEM((nf - 1, wrows, model), BF16),
+            pltpu.VMEM((3, wrows, model), BF16),
+            pltpu.VMEM((3, wrows, model), BF16),
             pltpu.VMEM((2, half, wrows, wide), BF16),
             pltpu.VMEM((half, wrows, wide), BF16),
             pltpu.VMEM((2, half - 1, wrows, wide), BF16),
             pltpu.SemaphoreType.DMA((pieces, 4)),
             pltpu.SemaphoreType.DMA((pieces, 4)),
-            pltpu.SemaphoreType.DMA((nf - 1,)),
-            pltpu.SemaphoreType.DMA((nf - 1,)),
-            pltpu.SemaphoreType.DMA((nf - 1,)),
-            pltpu.SemaphoreType.DMA((nf - 1,)),
+            pltpu.SemaphoreType.DMA((3,)),
+            pltpu.SemaphoreType.DMA((3,)),
+            pltpu.SemaphoreType.DMA((3,)),
+            pltpu.SemaphoreType.DMA((3,)),
             pltpu.SemaphoreType.DMA((2,)),
             pltpu.SemaphoreType.DMA((half - 1,)),
             pltpu.SemaphoreType.DMA((half - 1,)),

time: 195 us -> 193 us (0.990)
  no operation moved by 1% of the time
where the time goes in v3:
time: 193 us
  Pallas kernels  182 us (94%)
  local copies, waits for them, and re-layouts  8.57 us (4%)
    pallas_call x1, Pallas kernels, on_device(): pl.pallas_call(functools.partial(fused_kernel, heads, 1.0 / math.sqrt(tok...  182 us
    unnamed x12, local copies, waits for them, and re-layouts  5.59 us

profile of v3, /device:TPU:0, one launch (start us, length us, event | category | flops | bytes accessed | tf_op | source)
XLA Modules:
  0.0 192.7 jit_solution(9027705222155088669)
XLA Ops:
  1.3 0.8 slice_bitcast_fusion.1
  2.1 0.1 and_reduce_fusion
  2.2 0.1 copy.23
  2.3 0.9 add_select_fusion.1
  3.3 0.1 broadcast_in_dim.8
  3.3 0.6 copy.28
  4.0 0.4 copy.22
  4.3 0.3 copy.27
  4.6 1.1 pad_bitcast_fusion.wcol_ref
  5.7 0.6 pad.4.clone.wrow_ref
  6.3 181.7 %fused.1 = (bf16[384,1024]{1,0:T(8,128)(2,1)}, bf16[384,1024]{1,0:T(8,128)(2,1)}, bf16[384,1024]{1,0:T(8,128)(2,1)}, f32[256,256]{1,0:T(8,128)}) custom-call(f32[8]{0:T(128)} %slopes_ref.1, bf16[384,1024]{1,0:T(8,128)(2,1)} %bitcast.27, bf16[384,1024]{1,0:T(8,128)(2,1)} %bitcast.28, bf16[384,1024]{1,0:T(8,128)(2,1)} %bitcast.29, bf16[384,2048]{1,0:T(8,128)(2,1)} %bitcast.26, ...), custom_call_target="tpu_custom_call" | custom-call | flops 15099494400 | bytes 419430400 | tf_op jit(solution)/shard_map/fused/pallas_call | solution.py:453
  188.0 0.0 copy-start.1
  188.0 0.0 copy-start
  188.0 2.2 %copy.34 = bf16[1,384,1024]{2,1,0:T(8,128)(2,1)} copy(bf16[1,384,1024]{2,1,0:T(8,128)(2,1)} %bitcast.22) | data formatting | bytes 1572864
  190.2 0.0 copy-done.1
  190.2 0.0 copy-start.2
  190.2 0.9 copy.35
  191.1 0.0 copy-done
  191.1 0.9 copy.36
  192.0 0.0 copy-done.2
  192.0 0.7 copy.37
  (7 shorter events, 0.1 us)
Async XLA Ops:
  188.0 2.2 %copy-start.1 = (bf16[384,1024]{1,0:T(8,128)(2,1)S(1)}, bf16[384,1024]{1,0:T(8,128)(2,1)}, u32[]{:S(2)}) copy-start(bf16[384,1024]{1,0:T(8,128)(2,1)} %get-tuple-element.9) | copy-start | bytes 2359300
  188.0 3.1 %copy-start = (bf16[384,1024]{1,0:T(8,128)(2,1)S(1)}, bf16[384,1024]{1,0:T(8,128)(2,1)}, u32[]{:S(2)}) copy-start(bf16[384,1024]{1,0:T(8,128)(2,1)} %get-tuple-element.10) | copy-start | bytes 2359300
  190.2 1.8 copy-start.2
